TPU v7x, 256 devices: a whole 4x4x8 slice. The times are simulated.
256 devices in a mesh: grp: 8 (over z), pair: 32 (over x, y, core).
Axes of the slice: x: 4, y: 4, z: 8, core: 2. Of those that a mesh axis runs over, the one named last changes fastest.
Arguments:
- three_center: bfloat16 [512, 1024, 1024], P('pair', 'grp'), may hold values from -6 to 6
- virt_density: bfloat16 [1024, 1024], P(None, 'pair'), may hold values from -0.1875 to 0.1875
- occ_density: bfloat16 [1024, 1024], P(None, 'pair'), may hold values from -0.1875 to 0.1875
- tensor_mask: int32 [4, 8, 8], replicated, may hold values 0 or 1
- virt_mask: int32 [8, 8], replicated, may hold values 0 or 1
- occ_mask: int32 [8, 8], replicated, may hold values 0 or 1
- panel_order: int32 [512], replicated, may hold values from 0 to 511, each once
Outputs:
- response: float32 [512, 512], P(('grp', 'pair'))
Inputs may be any that keep to these rules, and one draw needn't show every extreme that they name: `tensor_mask`: each block is 0 (absent) or 1 (present). `virt_mask`: each block is 0 (absent) or 1 (present). `occ_mask`: each block is 0 (absent) or 1 (present). `panel_order`: every auxiliary index appears exactly once.
All inputs are finite; a program needn't handle non-finite values.
Results may differ from a plain program's by a relative error of at most 0.0041.
Values may be sent and summed in bfloat16 or wider, within the bound.
No kernel may reach another device: no remote copies, remote signals or barrier semaphores. Data moves between devices by JAX's collectives and lax.ppermute only.
A program may use at most 128 MiB of HBM per device.

v0:
```python
import jax
import jax.numpy as jnp
from jax import lax
from jax.sharding import PartitionSpec as P

NORB = 1024
BLK = 128


def spread_blocks(table):
    return jnp.repeat(jnp.repeat(table, BLK, axis=0), BLK, axis=1)


def density_local(density, mask_table, offset):
    full_mask = spread_blocks(mask_table).astype(jnp.bfloat16)
    local_mask = lax.dynamic_slice_in_dim(full_mask, offset, density.shape[1], 1)
    return density * local_mask


def per_device(
    three_center, virt_density, occ_density, tensor_mask, virt_mask, occ_mask, panel_order
):
    slab_rows, section_rows, orbitals = three_center.shape
    column_count = virt_density.shape[1]
    column_start = lax.axis_index("pair") * column_count
    aux_start = lax.axis_index("pair") * slab_rows
    row_block = (aux_start + jnp.arange(slab_rows, dtype=jnp.int32)) // BLK
    block_ids = jnp.arange(tensor_mask.shape[0], dtype=jnp.int32)
    selector = (row_block[:, None] == block_ids[None, :]).astype(jnp.float32)
    block_start = lax.axis_index("grp") * (section_rows // BLK)
    sub_mask = lax.dynamic_slice_in_dim(tensor_mask, block_start, section_rows // BLK, 1).astype(
        jnp.float32
    )
    row_mask = jnp.einsum("ab,bmn->amn", selector, sub_mask)
    row_mask = jnp.repeat(jnp.repeat(row_mask, BLK, axis=1), BLK, axis=2).astype(jnp.bfloat16)
    masked = three_center * row_mask
    virt_local = density_local(virt_density, virt_mask, column_start)
    occ_local = density_local(occ_density, occ_mask, column_start)
    half = jnp.einsum(
        "amn,ns->ams",
        masked,
        lax.all_gather(virt_local, "pair", axis=1, tiled=True),
        preferred_element_type=jnp.float32,
    ).astype(jnp.bfloat16)
    swapped = lax.all_to_all(half, "grp", split_axis=2, concat_axis=1, tiled=True)
    trans = jnp.einsum(
        "ams,ml->asl",
        swapped,
        lax.all_gather(occ_local, "pair", axis=1, tiled=True),
        preferred_element_type=jnp.float32,
    ).astype(jnp.bfloat16)
    owned_trans, owned_tensor = (
        lax.all_to_all(trans, "pair", split_axis=2, concat_axis=0, tiled=True),
        lax.all_to_all(masked, "pair", split_axis=2, concat_axis=0, tiled=True),
    )
    owned_trans = owned_trans.reshape(owned_trans.shape[0], -1)
    owned_tensor = owned_tensor.reshape(owned_tensor.shape[0], -1)
    picked = jnp.take(owned_trans, panel_order, axis=0)
    product = lax.dot_general(
        picked, owned_tensor, (((1,), (1,)), ((), ())), preferred_element_type=jnp.float32
    )
    return lax.psum_scatter(
        product * (1.0 / NORB), ("grp", "pair"), scatter_dimension=0, tiled=True
    )


def solution(mesh):
    placed = (P("pair", "grp", None), P(None, "pair"), P(None, "pair"), P(), P(), P(), P())
    return jax.shard_map(
        per_device, mesh=mesh, in_specs=placed, out_specs=P(("grp", "pair"), None), check_vma=False
    )
```

profile of v0, /device:TPU:2, one launch (start us, length us, event | category | flops | bytes accessed | tf_op | source)
XLA Modules:
  0.0 615.7 jit_solution(14071791125095684232)
XLA Ops:
  6.5 0.7 convert_element_type.43
  7.2 0.1 broadcast_bitcast_fusion.1
  7.3 0.3 broadcast_in_dim.36
  7.6 1.5 dynamic-slice_multiply_fusion.1
  9.1 6.9 %copy.18 = bf16[16,128,1024]{1,0,2:T(8,128)(2,1)} copy(bf16[16,128,1024]{2,1,0:T(8,128)(2,1)} %param.7) | data formatting | bytes 8388608 | tf_op args[0]
  16.0 0.7 dynamic-slice_convert_fusion
  16.8 0.2 convolution_convert_fusion.1
  17.0 5.8 broadcast_multiply_fusion
  22.8 38.3 %all-gather.3.cloned.1.call-done = bf16[1024,1024]{0,1:T(8,128)(2,1)} async-done(((bf16[1024,32]{0,1:T(8,128)(2,1)}), bf16[1024,1024]{0,1:T(8,128)(2,1)}) %all-gather.3.cloned.1.call-update) | async-done | bytes 2097168 | tf_op jit(solution)/shard_map/all_gather | solution.py:42
  61.1 9.6 %fusion.5 = bf16[16,128,1024]{2,1,0:T(8,128)(2,1)} fusion(bf16[16,128,1024]{1,0,2:T(8,128)(2,1)} %broadcast_multiply_fusion, bf16[1024,1024]{0,1:T(8,128)(2,1)} %all-gather.3.cloned.1.call-done), kind=kOutput, calls=%fused_computation.7 | convolution fusion | flops 4297064448 | bytes 10485760 | tf_op jit(solution)/shard_map/amn,ns->ams/dot_general | solution.py:39
  70.7 6.9 %copy.20 = bf16[16,128,1024]{1,0,2:T(8,128)(2,1)} copy(bf16[16,128,1024]{2,1,0:T(8,128)(2,1)} %fusion.5) | data formatting | bytes 8388608 | tf_op jit(solution)/shard_map/convert_element_type | solution.py:44
  77.7 7.1 %all-to-all-start = ((bf16[16,128,1024]{1,0,2:T(8,128)(2,1)}), bf16[16,128,1024]{1,0,2:T(8,128)(2,1)}, u32[]{:S(2)}, u32[]{:S(2)}) async-start(bf16[16,128,1024]{1,0,2:T(8,128)(2,1)} %copy.20), calls=%async_computation | async-start | bytes 8388608 | tf_op jit(solution)/shard_map/all_to_all | solution.py:45
  84.9 0.3 broadcast_in_dim.38
  85.2 0.6 dynamic-slice_multiply_fusion
  85.9 95.7 %all-to-all-done = bf16[16,128,1024]{1,0,2:T(8,128)(2,1)} async-done(((bf16[16,128,1024]{1,0,2:T(8,128)(2,1)}), bf16[16,128,1024]{1,0,2:T(8,128)(2,1)}, u32[]{:S(2)}, u32[]{:S(2)}) %all-to-all-start) | async-done | bytes 4194336 | tf_op jit(solution)/shard_map/all_to_all | solution.py:45
  181.6 5.9 all-to-all-start.2
  187.5 6.9 %copy.34 = bf16[16,128,8,128]{1,2,3,0:T(8,128)(2,1)} copy(bf16[16,128,8,128]{1,0,3,2:T(8,128)(2,1)} %bitcast.5) | data formatting | bytes 8388608 | tf_op jit(solution)/shard_map/all_to_all | solution.py:45
  194.4 7.3 %all_to_all.38 = bf16[16,1024,128]{1,2,0:T(8,128)(2,1)} reshape(bf16[16,8,128,128]{2,1,3,0:T(8,128)(2,1)} %bitcast.35) | data formatting | bytes 8388608 | tf_op jit(solution)/shard_map/all_to_all | solution.py:45
  201.7 9.4 %convolution_convert_fusion = bf16[16,128,1024]{2,1,0:T(8,128)(2,1)} fusion(bf16[16,1024,128]{1,2,0:T(8,128)(2,1)} %all_to_all.38, bf16[1024,1024]{0,1:T(8,128)(2,1)} %all-gather.5.cloned.1.call-done), kind=kOutput, calls=%fused_computation.8 | convolution fusion | flops 4297064448 | bytes 10485760 | tf_op jit(solution)/shard_map/ams,ml->asl/dot_general | solution.py:46
  211.1 6.9 %copy.22 = bf16[16,128,1024]{1,0,2:T(8,128)(2,1)} copy(bf16[16,128,1024]{2,1,0:T(8,128)(2,1)} %convolution_convert_fusion) | data formatting | bytes 8388608 | tf_op jit(solution)/shard_map/convert_element_type | solution.py:51
  217.9 19.2 %all-to-all-done.2 = bf16[16,128,1024]{1,0,2:T(8,128)(2,1)} async-done(((bf16[16,128,1024]{1,0,2:T(8,128)(2,1)}), bf16[16,128,1024]{1,0,2:T(8,128)(2,1)}, u32[]{:S(2)}, u32[]{:S(2)}) %all-to-all-start.2) | async-done | bytes 4194336 | tf_op jit(solution)/shard_map/all_to_all | solution.py:54
  237.2 9.6 %all-to-all-start.1 = ((bf16[16,128,1024]{1,0,2:T(8,128)(2,1)}), bf16[16,128,1024]{1,0,2:T(8,128)(2,1)}, u32[]{:S(2)}, u32[]{:S(2)}) async-start(bf16[16,128,1024]{1,0,2:T(8,128)(2,1)} %copy.22), calls=%async_computation.1 | async-start | bytes 8388608 | tf_op jit(solution)/shard_map/all_to_all | solution.py:53
  246.7 0.3 all-reduce.3.cloned.1.call-start
  247.0 14.6 %copy.26 = bf16[32,16,128,32]{3,2,1,0:T(8,128)(2,1)} copy(bf16[32,16,128,32]{2,1,3,0:T(8,128)(2,1)} %bitcast.15) | data formatting | bytes 8388608 | tf_op jit(solution)/shard_map/all_to_all | solution.py:54
  261.6 21.7 %reshape.50 = bf16[512,4096]{1,0:T(8,128)(2,1)} reshape(bf16[32,16,128,32]{3,2,1,0:T(8,128)(2,1)} %copy.26) | data formatting | bytes 8388608 | tf_op jit(solution)/shard_map/reshape | solution.py:57
  283.3 13.4 %all-to-all-done.1 = bf16[16,128,1024]{1,0,2:T(8,128)(2,1)} async-done(((bf16[16,128,1024]{1,0,2:T(8,128)(2,1)}), bf16[16,128,1024]{1,0,2:T(8,128)(2,1)}, u32[]{:S(2)}, u32[]{:S(2)}) %all-to-all-start.1) | async-done | bytes 4194336 | tf_op jit(solution)/shard_map/all_to_all | solution.py:53
  296.7 14.5 %copy.24 = bf16[32,16,128,32]{3,2,1,0:T(8,128)(2,1)} copy(bf16[32,16,128,32]{2,1,3,0:T(8,128)(2,1)} %bitcast.12) | data formatting | bytes 8388608 | tf_op jit(solution)/shard_map/all_to_all | solution.py:53
  311.2 21.7 %reshape.49 = bf16[512,4096]{1,0:T(8,128)(2,1)} reshape(bf16[32,16,128,32]{3,2,1,0:T(8,128)(2,1)} %copy.24) | data formatting | bytes 8388608 | tf_op jit(solution)/shard_map/reshape | solution.py:56
  332.9 11.3 %gather_fusion = bf16[512,4096]{1,0:T(8,128)(2,1)} fusion(bf16[512,4096]{1,0:T(8,128)(2,1)} %reshape.49, s32[1024]{0:T(1024)S(1)} %pad_clamp_fusion), kind=kCustom, calls=%fused_computation | custom fusion | bytes 8390656 | tf_op jit(solution)/shard_map/jit(_take)/gather | solution.py:58
  344.2 6.8 %fusion.11 = f32[512,512]{1,0:T(8,128)} fusion(bf16[512,4096]{1,0:T(8,128)(2,1)} %reshape.50, bf16[512,4096]{1,0:T(8,128)(2,1)} %gather_fusion, pred[512]{0:T(512)(128)(4,1)S(1)} %compare_and_fusion), kind=kOutput, calls=%fused_computation.13 | convolution fusion | flops 2149842944 | bytes 9437696 | tf_op jit(solution)/shard_map/dot_general | solution.py:59
  351.1 256.8 %all-reduce.3.cloned.1.call-done = f32[512,512]{1,0:T(8,128)} async-done(((f32[512,512]{1,0:T(8,128)}), f32[512,512]{1,0:T(8,128)}) %all-reduce.3.cloned.1.call-update) | async-done | bytes 1048592
  607.8 1.3 constant_dynamic-slice_fusion
  (19 shorter events, 0.2 us)
Async XLA Ops:
  6.5 54.6 %all-gather.3.cloned.1.call-start = ((), (), s32[]{:S(2)}) async-start(), calls=%async_computation.3 | async-start | bytes 2162688 | tf_op jit(solution)/shard_map/all_gather | solution.py:42
  77.7 7.2 %copy-start.2 = (s32[8,8]{1,0:T(8,128)S(1)}, s32[8,8]{1,0:T(8,128)}, u32[]{:S(2)}) copy-start(s32[8,8]{1,0:T(8,128)} %param.12) | copy-start | bytes 772
  77.7 7.6 %copy-start = (bf16[1024,32]{0,1:T(8,128)(2,1)S(1)}, bf16[1024,32]{0,1:T(8,128)(2,1)}, u32[]{:S(2)}) copy-start(bf16[1024,32]{0,1:T(8,128)(2,1)} %param.9) | copy-start | bytes 196612
  77.7 103.9 %all-to-all-start = ((bf16[16,128,1024]{1,0,2:T(8,128)(2,1)}), bf16[16,128,1024]{1,0,2:T(8,128)(2,1)}, u32[]{:S(2)}, u32[]{:S(2)}) async-start(bf16[16,128,1024]{1,0,2:T(8,128)(2,1)} %copy.20), calls=%async_computation | async-start | bytes 8388608 | tf_op jit(solution)/shard_map/all_to_all | solution.py:45
  84.8 116.9 %all-gather.5.cloned.1.call-start = ((), (), s32[]{:S(2)}) async-start(), calls=%async_computation.4 | async-start | bytes 2162688 | tf_op jit(solution)/shard_map/all_gather | solution.py:49
  181.6 55.6 %all-to-all-start.2 = ((bf16[16,128,1024]{1,0,2:T(8,128)(2,1)}), bf16[16,128,1024]{1,0,2:T(8,128)(2,1)}, u32[]{:S(2)}, u32[]{:S(2)}) async-start(bf16[16,128,1024]{1,0,2:T(8,128)(2,1)} %broadcast_multiply_fusion), calls=%async_computation.2 | async-start | bytes 8388608 | tf_op jit(solution)/shard_map/all_to_all | solution.py:54
  217.9 29.1 %copy-start.1 = (s32[512]{0:T(512)S(1)}, s32[512]{0:T(512)}, u32[]{:S(2)}) copy-start(s32[512]{0:T(512)} %param.13) | copy-start | bytes 6148
  237.2 59.5 %all-to-all-start.1 = ((bf16[16,128,1024]{1,0,2:T(8,128)(2,1)}), bf16[16,128,1024]{1,0,2:T(8,128)(2,1)}, u32[]{:S(2)}, u32[]{:S(2)}) async-start(bf16[16,128,1024]{1,0,2:T(8,128)(2,1)} %copy.22), calls=%async_computation.1 | async-start | bytes 8388608 | tf_op jit(solution)/shard_map/all_to_all | solution.py:53
  246.7 361.1 %all-reduce.3.cloned.1.call-start = ((), (), s32[]{:S(2)}) async-start(), calls=%async_computation.5 | async-start | bytes 2097152
Sparse Core Ops, SparseCore 0:
  9.9 51.1 all-gather.2
  88.2 48.0 all-gather.4
  351.2 256.6 all-reduce.2
where the time goes:
time: 618 us; the launch traced here: 616 us
  waiting for transfers between devices  423 us (68%)
  local copies, waits for them, and re-layouts  121 us (20%)
  matrix products  26 us (4%)
  starting transfers between devices  22.9 us (4%)
  between operations  13.2 us (2%)
  other arithmetic  9.4 us (2%)
    unnamed x4, waiting for transfers between devices  257 us
    all_to_all x1, waiting for transfers between devices, per_device(): lax.all_to_all(half, 'grp', split_axis=2, concat_axis=1, tiled=True)  95.7 us
    all_gather x1, waiting for transfers between devices, per_device(): lax.all_gather(virt_local, 'pair', axis=1, tiled=True)  38.3 us
    reshape x1, local copies, waits for them, and re-layouts, per_device(): owned_trans = owned_trans.reshape(owned_trans.shape[0], -1)  21.7 us
    reshape x1, local copies, waits for them, and re-layouts, per_device(): owned_tensor = owned_tensor.reshape(owned_tensor.shape[0], -1)  21.7 us
    all_to_all x1, waiting for transfers between devices, per_device(): lax.all_to_all(masked, 'pair', split_axis=2, concat_axis=0, tiled=True)  19.2 us
    all_to_all x1, local copies, waits for them, and re-layouts, per_device(): lax.all_to_all(masked, 'pair', split_axis=2, concat_axis=0, tiled=True)  14.6 us
    all_to_all x1, local copies, waits for them, and re-layouts, per_device(): lax.all_to_all(trans, 'pair', split_axis=2, concat_axis=0, tiled=True)  14.5 us
  transfers between devices with their start and end apart: 6, of which 5 were waited for; matrix products, arithmetic and copies ran while one was open for 12% of the time, Pallas kernels for 0%

commit v1 on v0

v1 whole, which is shorter than its diff:
```python
import functools

import jax
import jax.numpy as jnp
from jax import lax
from jax.experimental import pallas as pl
from jax.experimental.pallas import tpu as pltpu
from jax.sharding import PartitionSpec as P

NAUX = 512
NORB = 1024
BLK = 128
GRP = 8
PAIR = 32
AUX = NAUX // PAIR
SEC = NORB // GRP
COLS = NORB // PAIR
CHIPS = PAIR // 2
OWN = SEC // PAIR

SAME_CORE = [[core + 2 * chip for chip in range(CHIPS)] for core in range(2)]
PARTNER = [(i, i ^ 1) for i in range(PAIR)]
NT = (((1,), (1,)), ((), ()))
SMEM = pl.BlockSpec(memory_space=pltpu.SMEM)


def masked_rows(rows, keep):
    parts = []
    for b in range(NORB // BLK):
        part = rows[:, b * BLK : (b + 1) * BLK]
        parts.append(jnp.where(keep(b) != 0, part, jnp.zeros_like(part)))
    return jnp.concatenate(parts, axis=1)


S_TILE = 256


def half_kernel(place, virt_mask, tensor_mask, own, other, tensor, out, virt):
    core, table = place[0], place[1]
    tile = pl.program_id(0)
    chips = S_TILE // (2 * COLS)
    for c in range(chips):
        block = (tile * S_TILE + c * 2 * COLS) // BLK

        def keep(b):
            return virt_mask[b, block] * tensor_mask[table, b]

        mine = pl.multiple_of((2 * c + core) * COLS, COLS)
        theirs = pl.multiple_of((2 * c + 1 - core) * COLS, COLS)
        virt[pl.ds(mine, COLS), :] = masked_rows(own[c], keep)
        virt[pl.ds(theirs, COLS), :] = masked_rows(other[c], keep)
    half = lax.dot_general(virt[...], tensor[...], NT, preferred_element_type=jnp.float32)
    half = half.astype(jnp.bfloat16)
    by_aux = jnp.stack([half[:, a * SEC : (a + 1) * SEC] for a in range(AUX)], axis=0)
    out[...] = jnp.swapaxes(by_aux, 0, 1)


def half_transform(place, virt_mask, tensor_mask, own, other, tensor):
    chips = S_TILE // (2 * COLS)
    return pl.pallas_call(
        half_kernel,
        out_shape=jax.ShapeDtypeStruct((NORB, AUX, SEC), jnp.bfloat16),
        grid=(NORB // S_TILE,),
        in_specs=[
            SMEM,
            SMEM,
            SMEM,
            pl.BlockSpec((chips, COLS, NORB), lambda i: (i, 0, 0)),
            pl.BlockSpec((chips, COLS, NORB), lambda i: (i, 0, 0)),
            pl.BlockSpec((AUX * SEC, NORB), lambda i: (0, 0)),
        ],
        out_specs=pl.BlockSpec((S_TILE, AUX, SEC), lambda i: (i, 0, 0)),
        scratch_shapes=[pltpu.VMEM((S_TILE, NORB), jnp.bfloat16)],
        name="half_transform",
    )(place, virt_mask, tensor_mask, own, other, tensor)


M_TILE = 256


def turn_kernel(place, occ_mask, tensor_mask, own, other, tensor, out, occ):
    core, table = place[0], place[1]
    tile = pl.program_id(0)

    for c in range(CHIPS):
        block = c * 2 * COLS // BLK
        for rows, at in ((own, 2 * c + core), (other, 2 * c + 1 - core)):
            parts = []
            for b in range(M_TILE // BLK):
                part = rows[c, :, b * BLK : (b + 1) * BLK]
                live = occ_mask[tile * (M_TILE // BLK) + b, block] * tensor_mask[table, block]
                parts.append(jnp.where(live != 0, part, jnp.zeros_like(part)))
            occ[pl.ds(pl.multiple_of(at * COLS, COLS), COLS), :] = jnp.concatenate(parts, axis=1)

    turned = lax.dot_general(
        tensor[...], occ[...], (((1,), (0,)), ((), ())), preferred_element_type=jnp.float32
    )
    turned = turned.astype(jnp.bfloat16).reshape(AUX, SEC, M_TILE)
    out[...] = jnp.swapaxes(turned, 0, 1)


def turn_transform(place, occ_mask, tensor_mask, own, other, tensor):
    return pl.pallas_call(
        turn_kernel,
        out_shape=jax.ShapeDtypeStruct((SEC, AUX, NORB), jnp.bfloat16),
        grid=(NORB // M_TILE,),
        in_specs=[
            SMEM,
            SMEM,
            SMEM,
            pl.BlockSpec((CHIPS, COLS, M_TILE), lambda i: (0, 1, i)),
            pl.BlockSpec((CHIPS, COLS, M_TILE), lambda i: (0, 1, i)),
            pl.BlockSpec((AUX * SEC, NORB), lambda i: (0, 0)),
        ],
        out_specs=pl.BlockSpec((SEC, AUX, M_TILE), lambda i: (0, 0, i)),
        scratch_shapes=[pltpu.VMEM((NORB, M_TILE), jnp.bfloat16)],
        name="turn_transform",
    )(place, occ_mask, tensor_mask, own, other, tensor)


def response_kernel(order, left, right, out, total):
    step = pl.program_id(0)
    lhs = jnp.concatenate([left[g, :, 0].reshape(NAUX, SEC) for g in range(GRP)], axis=1)
    rhs = right[:, 0].reshape(NAUX, NORB)
    part = lax.dot_general(lhs, rhs, NT, preferred_element_type=jnp.float32)

    @pl.when(step == 0)
    def _():
        total[...] = part

    @pl.when(step > 0)
    def _():
        total[...] += part

    @pl.when(step == pl.num_programs(0) - 1)
    def _():
        rounded = (total[...] * (1.0 / NORB)).astype(jnp.bfloat16)
        columns = lax.broadcasted_iota(jnp.int32, (NAUX, NAUX), 1)
        pick = (order[...] == columns).astype(jnp.float32).astype(jnp.bfloat16)
        picked = jnp.dot(pick, rounded, preferred_element_type=jnp.float32)
        out[...] = picked.astype(jnp.bfloat16)


def partial_response(order, left, right):
    return pl.pallas_call(
        response_kernel,
        out_shape=jax.ShapeDtypeStruct((NAUX, NAUX), jnp.bfloat16),
        grid=(OWN,),
        in_specs=[
            pl.BlockSpec((NAUX, 1), lambda j: (0, 0)),
            pl.BlockSpec((GRP, PAIR, 1, AUX, SEC), lambda j: (0, 0, j, 0, 0)),
            pl.BlockSpec((PAIR, 1, AUX, NORB), lambda j: (0, j, 0, 0)),
        ],
        out_specs=pl.BlockSpec((NAUX, NAUX), lambda j: (0, 0)),
        scratch_shapes=[pltpu.VMEM((NAUX, NAUX), jnp.float32)],
        name="partial_response",
    )(order, left, right)


def per_device(
    three_center, virt_density, occ_density, tensor_mask, virt_mask, occ_mask, panel_order
):
    pair, grp = lax.axis_index("pair"), lax.axis_index("grp")
    tensor = three_center.reshape(AUX * SEC, NORB)
    table_rows = tensor_mask.reshape(-1, NORB // BLK)
    table = (pair * AUX // BLK) * (NORB // BLK) + grp
    place = jnp.stack([pair % 2, table]).astype(jnp.int32)

    shard = jnp.concatenate([virt_density.T, occ_density.T], axis=0)
    own = lax.all_to_all(
        jnp.broadcast_to(shard[None], (CHIPS, 2 * COLS, NORB)),
        "pair",
        0,
        0,
        axis_index_groups=SAME_CORE,
        tiled=True,
    )
    other = lax.ppermute(own, "pair", PARTNER)

    half = half_transform(place, virt_mask, table_rows, own, other, tensor)
    half = half.reshape(GRP * PAIR, OWN * AUX, SEC)
    left = lax.all_to_all(half, ("grp", "pair"), 0, 0, tiled=True)
    turned = turn_transform(place, occ_mask, table_rows, own, other, tensor)
    turned = turned.reshape(PAIR, OWN * AUX, NORB)
    right = lax.all_to_all(turned, "pair", 0, 0, tiled=True)

    order = panel_order.reshape(GRP, PAIR, 2).transpose(1, 0, 2).reshape(NAUX, 1)
    product = partial_response(
        order,
        left.reshape(GRP, PAIR, OWN, AUX, SEC),
        right.reshape(PAIR, OWN, AUX, NORB),
    )
    rows = lax.all_to_all(product.reshape(PAIR, AUX, NAUX), "pair", 0, 0, tiled=True)
    rows = jnp.sum(rows.astype(jnp.float32), axis=0).reshape(GRP, 2, NAUX)
    rows = lax.all_to_all(rows, "grp", 0, 0, tiled=True)
    return jnp.sum(rows, axis=0)


def solution(mesh):
    placed = (P("pair", "grp", None), P(None, "pair"), P(None, "pair"), P(), P(), P(), P())
    return jax.shard_map(
        per_device, mesh=mesh, in_specs=placed, out_specs=P(("grp", "pair"), None), check_vma=False
    )
```

time: 618 us -> 256 us (0.41)
  waiting for transfers between devices: 423 us -> 140 us
  local copies, waits for them, and re-layouts: 121 us -> 1.32 us
  blocking collectives: 0 us -> 59.3 us
  Pallas kernels: 0 us -> 26.4 us
  matrix products: 26 us -> 0 us
  between operations: 13.2 us -> 0.06 us
  other arithmetic: 9.4 us -> 2.28 us
    unnamed x4 -> x0, waiting for transfers between devices: 257 us -> none
    all_to_all x0 -> x3, blocking collectives: none -> 59.3 us  [the longest x1 33.8 us: per_device(): lax.all_to_all(jnp.broadcast_to(shard[None], (CHIPS, 2 * COLS, NORB)), 'p...]
    all_to_all x4 -> x0, local copies, waits for them, and re-layouts: 43.3 us -> none  [the longest x1 14.6 us: per_device(): lax.all_to_all(masked, 'pair', split_axis=2, concat_axis=0, tiled=True)]
    reshape x2 -> x3, local copies, waits for them, and re-layouts: 43.4 us -> 0.98 us  [the longest x2 0.95 us: per_device(): panel_order.reshape(GRP, PAIR, 2).transpose(1, 0, 2).reshape(NAUX, 1)]
    all_gather x2 -> x0, waiting for transfers between devices: 38.3 us -> none  [the longest x1 38.3 us: per_device(): lax.all_gather(virt_local, 'pair', axis=1, tiled=True)]
    pallas_call x0 -> x3, Pallas kernels: none -> 26.4 us  [the longest x1 10.1 us: turn_transform(): pl.pallas_call(turn_kernel, out_shape=jax.ShapeDtypeStruct((SEC, AUX, NOR...]
    dot_general x4 -> x0, matrix products: 26 us -> none  [the longest x1 9.61 us: per_device(): jnp.einsum('amn,ns->ams', masked, lax.all_gather(virt_local, 'pair', axis...]
    convert_element_type x4 -> x0, local copies, waits for them, and re-layouts: 13.9 us -> none  [the longest x1 6.94 us: per_device(): half = jnp.einsum('amn,ns->ams', masked, lax.all_gather(virt_local, 'pair...]
  transfers between devices with their start and end apart: 6 -> 3, of which waited for: 5 -> 3; matrix products, arithmetic and copies ran while one was open for 12% -> 1% of each run, Pallas kernels for 0% -> 4%
where the time goes in v1:
time: 256 us; the launch traced here: 254 us
  waiting for transfers between devices  140 us (55%)
  blocking collectives  59.3 us (23%)
  Pallas kernels  26.4 us (10%)
  starting transfers between devices  23.9 us (9%)
    all_to_all x1, waiting for transfers between devices, per_device(): left = lax.all_to_all(half, ('grp', 'pair'), 0, 0, tiled=True)  96.3 us
    all_to_all x1, waiting for transfers between devices, per_device(): right = lax.all_to_all(turned, 'pair', 0, 0, tiled=True)  40.5 us
    all_to_all x1, blocking collectives, per_device(): lax.all_to_all(jnp.broadcast_to(shard[None], (CHIPS, 2 * COLS, NORB)), 'p...  33.8 us
    all_to_all x1, starting transfers between devices, per_device(): left = lax.all_to_all(half, ('grp', 'pair'), 0, 0, tiled=True)  17.6 us
    all_to_all x1, blocking collectives, per_device(): lax.all_to_all(product.reshape(PAIR, AUX, NAUX), 'pair', 0, 0, tiled=True)  14.7 us
    all_to_all x1, blocking collectives, per_device(): rows = lax.all_to_all(rows, 'grp', 0, 0, tiled=True)  10.9 us
    pallas_call x1, Pallas kernels, turn_transform(): pl.pallas_call(turn_kernel, out_shape=jax.ShapeDtypeStruct((SEC, AUX, NOR...  10.1 us
    pallas_call x1, Pallas kernels, half_transform(): pl.pallas_call(half_kernel, out_shape=jax.ShapeDtypeStruct((NORB, AUX, SE...  9.14 us
  transfers between devices with their start and end apart: 3, of which 3 were waited for; matrix products, arithmetic and copies ran while one was open for 1% of the time, Pallas kernels for 4%

profile of v1, /device:TPU:2, one launch (start us, length us, event | category | flops | bytes accessed | tf_op | source)
XLA Modules:
  0.0 253.7 jit_solution(9079378127854657070)
XLA Ops:
  0.0 0.9 pad_maximum_fusion
  0.9 0.3 broadcast_in_dim.2
  1.1 33.8 %all_to_all.25.own = bf16[16,64,1024]{2,1,0:T(8,128)(2,1)S(1)} all-to-all(bf16[16,64,1024]{2,1,0:T(8,128)(2,1)S(1)} %broadcast_in_dim.2), channel_id=1, replica_groups={{0,2,4,6,8,10,12,14,16,18,20,22,24,26,28,30},{1,3,5,7,9,11,13,15,17,19,..., dimensions={0} | all-to-all | bytes 4194304 | tf_op jit(solution)/shard_map/all_to_all | solution.py:170
  34.9 0.0 copy-start
  34.9 0.0 collective-permute-start
  34.9 0.7 pad_add_fusion.place
  35.6 3.6 %collective-permute-done.other = bf16[16,64,1024]{2,1,0:T(8,128)(2,1)} collective-permute-done((bf16[16,64,1024]{2,1,0:T(8,128)(2,1)S(1)}, bf16[16,64,1024]{2,1,0:T(8,128)(2,1)}, u32[]{:S(2)}, u32[]{:S(2)}) %collective-permute-start) | collective-permute-done | bytes 2097184 | tf_op jit(solution)/shard_map/ppermute | solution.py:178
  39.2 0.0 copy-done
  39.2 10.1 %turn_transform.1 = bf16[128,16,1024]{2,1,0:T(8,128)(2,1)} custom-call(s32[2]{0:T(128)} %pad_add_fusion.place, s32[8,8]{1,0:T(8,128)} %occ_mask.1, s32[32,8]{1,0:T(8,128)} %bitcast.18, bf16[16,64,1024]{2,1,0:T(8,128)(2,1)} %copy-done, bf16[16,64,1024]{2,1,0:T(8,128)(2,1)} %collective-permute-done.other, bf16[2048,1024]{1,0:T(8,128)(2,1)} %bitcast.12), custom_call_target="tpu_custom_call" | custom-call | tf_op jit(solution)/shard_map/turn_transform/pallas_call | solution.py:103
  49.3 6.3 %all-to-all-start.2 = ((bf16[32,64,1024]{2,1,0:T(8,128)(2,1)}), bf16[32,64,1024]{2,1,0:T(8,128)(2,1)}, u32[]{:S(2)}, u32[]{:S(2)}) async-start(bf16[32,64,1024]{2,1,0:T(8,128)(2,1)} %bitcast.15), calls=%async_computation.2 | async-start | bytes 8388608 | tf_op jit(solution)/shard_map/all_to_all | solution.py:185
  55.6 9.1 %half_transform.1 = bf16[1024,16,128]{2,1,0:T(8,128)(2,1)} custom-call(s32[2]{0:T(128)} %pad_add_fusion.place, s32[8,8]{1,0:T(8,128)} %virt_mask.1, s32[32,8]{1,0:T(8,128)} %bitcast.19, bf16[16,64,1024]{2,1,0:T(8,128)(2,1)} %copy-done, bf16[16,64,1024]{2,1,0:T(8,128)(2,1)} %collective-permute-done.other, bf16[2048,1024]{1,0:T(8,128)(2,1)} %bitcast.13), custom_call_target="tpu_custom_call" | custom-call | tf_op jit(solution)/shard_map/half_transform/pallas_call | solution.py:60
  64.8 40.5 %all-to-all-done.2 = bf16[32,64,1024]{2,1,0:T(8,128)(2,1)} async-done(((bf16[32,64,1024]{2,1,0:T(8,128)(2,1)}), bf16[32,64,1024]{2,1,0:T(8,128)(2,1)}, u32[]{:S(2)}, u32[]{:S(2)}) %all-to-all-start.2) | async-done | bytes 4194336 | tf_op jit(solution)/shard_map/all_to_all | solution.py:185
  105.3 0.0 copy-start.1
  105.3 17.6 %all-to-all-start.1 = ((bf16[256,64,128]{2,1,0:T(8,128)(2,1)}), bf16[256,64,128]{2,1,0:T(8,128)(2,1)}, u32[]{:S(2)}, u32[]{:S(2)}) async-start(bf16[256,64,128]{2,1,0:T(8,128)(2,1)} %bitcast.14), calls=%async_computation.1 | async-start | bytes 8388608 | tf_op jit(solution)/shard_map/all_to_all | solution.py:182
  122.9 0.0 copy-done.1
  122.9 0.1 reshape.31
  123.1 0.1 copy.12
  123.1 0.8 reshape.41.order
  124.0 96.3 %all-to-all-done.1 = bf16[256,64,128]{2,1,0:T(8,128)(2,1)} async-done(((bf16[256,64,128]{2,1,0:T(8,128)(2,1)}), bf16[256,64,128]{2,1,0:T(8,128)(2,1)}, u32[]{:S(2)}, u32[]{:S(2)}) %all-to-all-start.1) | async-done | bytes 4194336 | tf_op jit(solution)/shard_map/all_to_all | solution.py:182
  220.3 7.1 %partial_response.1 = bf16[512,512]{1,0:T(8,128)(2,1)} custom-call(s32[512,1]{1,0:T(8,128)} %reshape.41.order, bf16[8,32,4,16,128]{4,3,2,1,0:T(8,128)(2,1)} %bitcast.8.left, bf16[32,4,16,1024]{3,2,1,0:T(8,128)(2,1)} %bitcast.10.right), custom_call_target="tpu_custom_call" | custom-call | tf_op jit(solution)/shard_map/partial_response/pallas_call | solution.py:145
  227.4 14.7 %all_to_all.26 = bf16[32,16,512]{2,1,0:T(8,128)(2,1)S(1)} all-to-all(bf16[32,16,512]{2,1,0:T(8,128)(2,1)} %bitcast.16), channel_id=1, replica_groups=mesh['grp'=8,'pair'=32] {'pair'}, dimensions={0} | all-to-all | bytes 1048576 | tf_op jit(solution)/shard_map/all_to_all | solution.py:193
  242.1 0.1 convert_reduce_fusion
  242.2 10.9 %all_to_all.27 = f32[8,2,512]{2,1,0:T(2,128)S(1)} all-to-all(f32[8,2,512]{2,1,0:T(2,128)S(1)} %reshape.40), channel_id=1, replica_groups=mesh['grp'=8,'pair'=32] {'grp'}, dimensions={0} | all-to-all | bytes 65536 | tf_op jit(solution)/shard_map/all_to_all | solution.py:195
  253.1 0.6 reduce_sum.19
  (1 shorter events, 0.0 us)
Async XLA Ops:
  34.9 4.3 %copy-start = (bf16[16,64,1024]{2,1,0:T(8,128)(2,1)}, bf16[16,64,1024]{2,1,0:T(8,128)(2,1)S(1)}, u32[]{:S(2)}) copy-start(bf16[16,64,1024]{2,1,0:T(8,128)(2,1)S(1)} %all_to_all.25.own) | copy-start | bytes 6291460
  34.9 4.3 %collective-permute-start = (bf16[16,64,1024]{2,1,0:T(8,128)(2,1)S(1)}, bf16[16,64,1024]{2,1,0:T(8,128)(2,1)}, u32[]{:S(2)}, u32[]{:S(2)}) collective-permute-start(bf16[16,64,1024]{2,1,0:T(8,128)(2,1)S(1)} %all_to_all.25.own), channel_id=1, source_target_pairs={{0,1},{1,0},{2,3},{3,2},{4,5},{5,4},{6,7},{7,6},{8,9},{9,8},{10,11... | collective-permute-start | bytes 6291464 | tf_op jit(solution)/shard_map/ppermute | solution.py:178
  49.3 56.0 %all-to-all-start.2 = ((bf16[32,64,1024]{2,1,0:T(8,128)(2,1)}), bf16[32,64,1024]{2,1,0:T(8,128)(2,1)}, u32[]{:S(2)}, u32[]{:S(2)}) async-start(bf16[32,64,1024]{2,1,0:T(8,128)(2,1)} %bitcast.15), calls=%async_computation.2 | async-start | bytes 8388608 | tf_op jit(solution)/shard_map/all_to_all | solution.py:185
  105.3 17.6 %copy-start.1 = (s32[512]{0:T(512)S(1)}, s32[512]{0:T(512)}, u32[]{:S(2)}) copy-start(s32[512]{0:T(512)} %param.13) | copy-start | bytes 6148
  105.3 115.0 %all-to-all-start.1 = ((bf16[256,64,128]{2,1,0:T(8,128)(2,1)}), bf16[256,64,128]{2,1,0:T(8,128)(2,1)}, u32[]{:S(2)}, u32[]{:S(2)}) async-start(bf16[256,64,128]{2,1,0:T(8,128)(2,1)} %bitcast.14), calls=%async_computation.1 | async-start | bytes 8388608 | tf_op jit(solution)/shard_map/all_to_all | solution.py:182
